TPU v7x, 256 devices: a whole 4x4x8 slice. The times are simulated.
256 devices in a mesh: mp: 32 (over z, y_hi, core), dp: 8 (over x, y_lo).
Axes of the slice: x: 4, y: 4 (y_hi: 2, y_lo: 2; y = y_hi * 2 + y_lo), z: 8, core: 2. Of those that a mesh axis runs over, the one named last changes fastest.
Arguments:
- tokens: bfloat16 [1024, 8192], P('mp', 'dp'), may hold values from -6 to 6
- gate_weight: bfloat16 [8192, 16384], P('dp', 'mp'), may hold values from -0.0625 to 0.0625
- up_weight: bfloat16 [8192, 16384], P('dp', 'mp'), may hold values from -0.0625 to 0.0625
- down_weight: bfloat16 [16384, 8192], P('mp', 'dp'), may hold values from -0.046875 to 0.046875
- cotangent: bfloat16 [1024, 8192], P('mp', 'dp'), may hold values from -6 to 6
Outputs:
- mixed: bfloat16 [1024, 8192], P('mp', 'dp')
- token_grad: bfloat16 [1024, 8192], P('mp', 'dp')
- gate_grad: bfloat16 [8192, 16384], P('dp', 'mp')
- up_grad: bfloat16 [8192, 16384], P('dp', 'mp')
- down_grad: bfloat16 [16384, 8192], P('mp', 'dp')
All inputs are finite; a program needn't handle non-finite values.
Results may differ from a plain program's by a relative error of at most 0.005.
Values may be sent and summed in bfloat16 or wider, within the bound.
No kernel may reach another device: no remote copies, remote signals or barrier semaphores. Data moves between devices by JAX's collectives and lax.ppermute only.
A program may use at most 64 MiB of HBM per device.

v0:
```python
import jax
import jax.numpy as jnp
from jax import lax
from jax.sharding import PartitionSpec as P


def contract_rows(left, right):
    return lax.dot_general(
        left, right, (((0,), (0,)), ((), ())), preferred_element_type=jnp.float32
    )


def contract_cols(left, right):
    return lax.dot_general(
        left, right, (((1,), (1,)), ((), ())), preferred_element_type=jnp.float32
    )


def body(tokens, gate_weight, up_weight, down_weight, cotangent):
    token_all = lax.all_gather(tokens, "mp", axis=0, tiled=True)
    width = gate_weight.shape[1]
    block = token_all
    first = jnp.dot(block, gate_weight, preferred_element_type=jnp.float32)
    second = jnp.dot(block, up_weight, preferred_element_type=jnp.float32)
    both = lax.psum(jnp.concatenate([first, second], axis=1), "dp")
    gate = both[:, :width]
    up = both[:, width:]
    sig = jax.nn.sigmoid(gate)
    act = gate * sig
    hidden_part = (act * up).astype(jnp.bfloat16)
    block = hidden_part
    mixed = lax.psum_scatter(
        jnp.dot(block, down_weight, preferred_element_type=jnp.float32),
        "mp",
        scatter_dimension=0,
        tiled=True,
    ).astype(jnp.bfloat16)
    cot_all = lax.all_gather(cotangent, "mp", axis=0, tiled=True)
    down_grad = contract_rows(hidden_part, cot_all).astype(jnp.bfloat16)
    block = cot_all
    hidden_back = lax.psum(contract_cols(block, down_weight), "dp")
    pre_gate = (hidden_back * up * sig * (1.0 + gate * (1.0 - sig))).astype(jnp.bfloat16)
    pre_up = (hidden_back * act).astype(jnp.bfloat16)
    gate_all, up_all = (pre_gate, pre_up)
    gate_grad = contract_rows(token_all, gate_all).astype(jnp.bfloat16)
    up_grad = contract_rows(token_all, up_all).astype(jnp.bfloat16)
    first = gate_all
    second = up_all
    token_grad = lax.psum_scatter(
        contract_cols(first, gate_weight) + contract_cols(second, up_weight),
        "mp",
        scatter_dimension=0,
        tiled=True,
    ).astype(jnp.bfloat16)
    return (mixed, token_grad, gate_grad, up_grad, down_grad)


def solution(mesh):
    in_specs = (P("mp", "dp"), P("dp", "mp"), P("dp", "mp"), P("mp", "dp"), P("mp", "dp"))
    out_specs = (P("mp", "dp"), P("mp", "dp"), P("dp", "mp"), P("dp", "mp"), P("mp", "dp"))
    return jax.shard_map(body, mesh=mesh, in_specs=in_specs, out_specs=out_specs, check_vma=False)
```

profile of v0, /device:TPU:6, one launch (start us, length us, event | category | flops | bytes accessed | tf_op | source)
XLA Modules:
  0.0 717.8 jit_solution(3119205423730051404)
XLA Ops:
  7.2 0.0 copy-start
  7.2 0.0 all-gather.3.cloned.1.call-start
  7.2 0.7 all-gather.3.cloned.1.call-update
  7.9 0.0 all-gather.5.cloned.1.call-start
  8.0 0.7 all-gather.5.cloned.1.call-update
  8.7 0.0 all-reduce.3.cloned.1.call-start
  8.7 84.9 %all-gather.3.cloned.1.call-done = bf16[1024,1024]{1,0:T(8,128)(2,1)} async-done(((bf16[32,1024]{1,0:T(8,128)(2,1)}), bf16[1024,1024]{1,0:T(8,128)(2,1)}) %all-gather.3.cloned.1.call-update) | async-done | bytes 2097168 | tf_op jit(solution)/shard_map/all_gather | solution.py:20
  93.6 0.0 copy-start.4
  93.6 3.3 fusion.4
  96.9 0.0 copy-done
  96.9 0.0 copy-done.4
  96.9 1.3 fusion.3
  98.2 0.0 copy-start.3
  98.2 2.5 pad_maximum_fusion
  100.7 72.0 %all-gather.5.cloned.1.call-done = bf16[1024,1024]{1,0:T(8,128)(2,1)} async-done(((bf16[32,1024]{1,0:T(8,128)(2,1)}), bf16[1024,1024]{1,0:T(8,128)(2,1)}) %all-gather.5.cloned.1.call-update) | async-done | bytes 2097168 | tf_op jit(solution)/shard_map/all_gather | solution.py:38
  172.7 0.0 copy-done.3
  172.7 4.2 fusion.6
  176.9 0.0 all-reduce.3.cloned.1.call-update
  176.9 0.0 reduce-scatter.5.cloned.1.call-start
  177.0 262.9 %all-reduce.3.cloned.1.call-done = (f32[1024,1024]{0,1:T(8,128)}, f32[1024,512]{0,1:T(8,128)}) async-done(((f32[1024,1024]{0,1:T(8,128)}, f32[1024,512]{0,1:T(8,128)}), (f32[1024,1024]{0,1:T(8,128)}, f32[1024,512]{0,1:T(8,128)})) %all-reduce.3.cloned.1.call-update) | async-done | bytes 6291472 | tf_op jit(solution)/shard_map/psum | solution.py:25
  439.9 4.3 multiply_convert_fusion
  444.2 0.0 copy-start.2
  444.2 0.0 copy-start.1
  444.2 1.3 fusion.7
  445.5 0.0 copy-done.2
  445.5 0.3 copy-done.1
  445.8 3.3 convolution_add_fusion
  449.1 0.0 reduce-scatter.5.cloned.1.call-update
  449.1 0.2 reduce-scatter.3.cloned.1.call-start
  449.3 4.5 fusion.5
  453.8 0.0 reduce-scatter.3.cloned.1.call-update
  453.8 4.1 fusion.1
  458.0 2.3 copy.11
  460.3 3.8 fusion.2
  464.1 2.3 copy.12
  466.4 3.9 convolution_convert_fusion
  470.2 109.2 %reduce-scatter.5.cloned.1.call-done = f32[32,1024]{1,0:T(8,128)} async-done(((f32[1024,1024]{1,0:T(8,128)}), f32[32,1024]{1,0:T(8,128)}) %reduce-scatter.5.cloned.1.call-update) | async-done | bytes 131088 | tf_op jit(solution)/shard_map/reduce_scatter | solution.py:49
  579.4 1.5 convert_element_type.34
  581.0 128.8 %reduce-scatter.3.cloned.1.call-done = f32[32,1024]{1,0:T(8,128)} async-done(((f32[1024,1024]{1,0:T(8,128)}), f32[32,1024]{1,0:T(8,128)}) %reduce-scatter.3.cloned.1.call-update) | async-done | bytes 131088 | tf_op jit(solution)/shard_map/reduce_scatter | solution.py:32
  709.8 1.5 convert_element_type.31
Async XLA Ops:
  7.2 89.7 %copy-start = (bf16[1024,512]{1,0:T(8,128)(2,1)S(1)}, bf16[1024,512]{1,0:T(8,128)(2,1)}, u32[]{:S(2)}) copy-start(bf16[1024,512]{1,0:T(8,128)(2,1)} %param.6) | copy-start | bytes 3145732
  7.2 86.4 %all-gather.3.cloned.1.call-start = ((), (), s32[]{:S(2)}) async-start(), calls=%async_computation.2 | async-start | bytes 2162688 | tf_op jit(solution)/shard_map/all_gather | solution.py:20
  7.9 164.8 %all-gather.5.cloned.1.call-start = ((), (), s32[]{:S(2)}) async-start(), calls=%async_computation.4 | async-start | bytes 2162688 | tf_op jit(solution)/shard_map/all_gather | solution.py:38
  8.7 431.2 %all-reduce.3.cloned.1.call-start = ((), (), s32[]{:S(2)}) async-start(), calls=%async_computation.6 | async-start | bytes 12582912 | tf_op jit(solution)/shard_map/psum | solution.py:25
  93.6 3.3 copy-start.4
  98.2 74.5 %copy-start.3 = (bf16[512,1024]{1,0:T(8,128)(2,1)S(1)}, bf16[512,1024]{1,0:T(8,128)(2,1)}, u32[]{:S(2)}) copy-start(bf16[512,1024]{1,0:T(8,128)(2,1)} %param.8) | copy-start | bytes 3145732
  176.9 402.5 %reduce-scatter.5.cloned.1.call-start = ((), (), s32[]{:S(2)}) async-start(), calls=%async_computation.5 | async-start | bytes 4325376 | tf_op jit(solution)/shard_map/reduce_scatter | solution.py:49
  444.2 1.3 copy-start.2
  444.2 1.6 copy-start.1
  449.1 260.7 %reduce-scatter.3.cloned.1.call-start = ((), (), s32[]{:S(2)}) async-start(), calls=%async_computation.3 | async-start | bytes 4325376 | tf_op jit(solution)/shard_map/reduce_scatter | solution.py:32
Sparse Core Ops, SparseCore 0:
  10.8 82.7 all-gather.2
  96.4 76.3 all-gather.4
  177.1 262.8 all-reduce.2
  449.2 130.1 reduce-scatter.4
  583.5 126.2 reduce-scatter.2
where the time goes:
time: 718 us
  waiting for transfers between devices  659 us (92%)
  matrix products  29.7 us (4%)
  between operations  13.9 us (2%)
  other arithmetic  9.84 us (1%)
    psum x1, waiting for transfers between devices, body(): both = lax.psum(jnp.concatenate([first, second], axis=1), 'dp')  263 us
    reduce_scatter x1, waiting for transfers between devices, body(): lax.psum_scatter(jnp.dot(block, down_weight, preferred_element_type=jnp.f...  129 us
    reduce_scatter x1, waiting for transfers between devices, body(): lax.psum_scatter(contract_cols(first, gate_weight) + contract_cols(second...  109 us
    all_gather x1, waiting for transfers between devices, body(): token_all = lax.all_gather(tokens, 'mp', axis=0, tiled=True)  84.9 us
    all_gather x1, waiting for transfers between devices, body(): cot_all = lax.all_gather(cotangent, 'mp', axis=0, tiled=True)  72 us
  transfers between devices with their start and end apart: 5, of which 5 were waited for; matrix products, arithmetic and copies ran while one was open for 4% of the time, Pallas kernels for 0%

commit v1 on v0

--- a/solution.py
+++ b/solution.py
@@ -35,7 +35,8 @@
         scatter_dimension=0,
         tiled=True,
     ).astype(jnp.bfloat16)
-    cot_all = lax.all_gather(cotangent, "mp", axis=0, tiled=True)
+    sent = jnp.stack([cotangent] * lax.axis_size("mp"))
+    cot_all = jnp.concatenate(lax.all_to_all(sent, "mp", 0, 0), axis=0)
     down_grad = contract_rows(hidden_part, cot_all).astype(jnp.bfloat16)
     block = cot_all
     hidden_back = lax.psum(contract_cols(block, down_weight), "dp")

time: 718 us -> 652 us (0.908)
  waiting for transfers between devices: 659 us -> 579 us
  starting transfers between devices: 0.38 us -> 11.8 us
    all_gather x1 -> x0, waiting for transfers between devices: 72 us -> none  [body(): cot_all = lax.all_gather(cotangent, 'mp', axis=0, tiled=True)]
    all_to_all x0 -> x1, starting transfers between devices: none -> 11.5 us  [body(): cot_all = jnp.concatenate(lax.all_to_all(sent, 'mp', 0, 0), axis=0)]
    all_gather x1, waiting for transfers between devices: 84.9 us -> 76.9 us  [body(): token_all = lax.all_gather(tokens, 'mp', axis=0, tiled=True)]
  transfers between devices with their start and end apart: 5 -> 5, of which waited for: 5 -> 4; matrix products, arithmetic and copies ran while one was open for 4% -> 5% of each run, Pallas kernels for 0% -> 0%
where the time goes in v1:
time: 652 us; the launch traced here: 651 us
  waiting for transfers between devices  579 us (89%)
  matrix products  30.1 us (5%)
  between operations  13.9 us (2%)
  starting transfers between devices  11.8 us (2%)
  other arithmetic  9.81 us (2%)
  local copies, waits for them, and re-layouts  7.29 us (1%)
    psum x1, waiting for transfers between devices, body(): both = lax.psum(jnp.concatenate([first, second], axis=1), 'dp')  263 us
    reduce_scatter x1, waiting for transfers between devices, body(): lax.psum_scatter(jnp.dot(block, down_weight, preferred_element_type=jnp.f...  129 us
    reduce_scatter x1, waiting for transfers between devices, body(): lax.psum_scatter(contract_cols(first, gate_weight) + contract_cols(second...  109 us
    all_gather x1, waiting for transfers between devices, body(): token_all = lax.all_gather(tokens, 'mp', axis=0, tiled=True)  76.9 us
  transfers between devices with their start and end apart: 5, of which 4 were waited for; matrix products, arithmetic and copies ran while one was open for 5% of the time, Pallas kernels for 0%

profile of v1, /device:TPU:6, one launch (start us, length us, event | category | flops | bytes accessed | tf_op | source)
XLA Modules:
  0.0 651.4 jit_solution(13296313691385874103)
XLA Ops:
  7.2 0.0 copy-start
  7.2 0.0 all-gather.2.cloned.1.call-start
  7.2 0.7 all-gather.2.cloned.1.call-update
  7.9 2.4 stack.2
  10.4 11.5 %all-to-all-start = ((bf16[32,32,1024]{2,1,0:T(8,128)(2,1)}), bf16[32,32,1024]{2,1,0:T(8,128)(2,1)S(1)}, u32[]{:S(2)}, u32[]{:S(2)}) async-start(bf16[32,32,1024]{2,1,0:T(8,128)(2,1)} %stack.2), calls=%async_computation.1 | async-start | bytes 4194304 | tf_op jit(solution)/shard_map/all_to_all | solution.py:39
  21.8 0.0 all-reduce.3.cloned.1.call-start
  21.9 76.9 %all-gather.2.cloned.1.call-done = bf16[1024,1024]{1,0:T(8,128)(2,1)} async-done(((bf16[32,1024]{1,0:T(8,128)(2,1)}), bf16[1024,1024]{1,0:T(8,128)(2,1)}) %all-gather.2.cloned.1.call-update) | async-done | bytes 2097168 | tf_op jit(solution)/shard_map/all_gather | solution.py:20
  98.8 0.0 copy-start.4
  98.8 3.3 fusion.4
  102.1 0.0 copy-done
  102.1 0.0 copy-done.4
  102.1 1.3 fusion.3
  103.5 2.5 pad_maximum_fusion
  105.9 0.0 all-to-all-done
  105.9 0.0 copy-start.1
  105.9 4.6 fusion.6
  110.5 0.0 copy-done.1
  110.5 0.0 all-reduce.3.cloned.1.call-update
  110.5 0.0 reduce-scatter.5.cloned.1.call-start
  110.6 262.9 %all-reduce.3.cloned.1.call-done = (f32[1024,1024]{0,1:T(8,128)}, f32[1024,512]{0,1:T(8,128)}) async-done(((f32[1024,1024]{0,1:T(8,128)}, f32[1024,512]{0,1:T(8,128)}), (f32[1024,1024]{0,1:T(8,128)}, f32[1024,512]{0,1:T(8,128)})) %all-reduce.3.cloned.1.call-update) | async-done | bytes 6291472 | tf_op jit(solution)/shard_map/psum | solution.py:25
  373.5 4.3 multiply_convert_fusion
  377.8 0.0 copy-start.3
  377.8 0.0 copy-start.2
  377.8 1.3 fusion.7
  379.1 0.0 copy-done.3
  379.1 0.3 copy-done.2
  379.4 3.3 convolution_add_fusion
  382.7 0.0 reduce-scatter.5.cloned.1.call-update
  382.7 0.2 reduce-scatter.3.cloned.1.call-start
  383.0 4.5 fusion.5
  387.4 0.0 reduce-scatter.3.cloned.1.call-update
  387.4 4.1 fusion.1
  391.6 2.3 copy.11
  393.9 3.8 fusion.2
  397.7 2.3 copy.12
  400.0 3.9 convolution_convert_fusion
  403.8 109.2 %reduce-scatter.5.cloned.1.call-done = f32[32,1024]{1,0:T(8,128)} async-done(((f32[1024,1024]{1,0:T(8,128)}), f32[32,1024]{1,0:T(8,128)}) %reduce-scatter.5.cloned.1.call-update) | async-done | bytes 131088 | tf_op jit(solution)/shard_map/reduce_scatter | solution.py:50
  513.0 1.5 convert_element_type.34
  514.6 128.7 %reduce-scatter.3.cloned.1.call-done = f32[32,1024]{1,0:T(8,128)} async-done(((f32[1024,1024]{1,0:T(8,128)}), f32[32,1024]{1,0:T(8,128)}) %reduce-scatter.3.cloned.1.call-update) | async-done | bytes 131088 | tf_op jit(solution)/shard_map/reduce_scatter | solution.py:32
  643.3 1.5 convert_element_type.31
Async XLA Ops:
  7.2 95.0 %copy-start = (bf16[1024,512]{1,0:T(8,128)(2,1)S(1)}, bf16[1024,512]{1,0:T(8,128)(2,1)}, u32[]{:S(2)}) copy-start(bf16[1024,512]{1,0:T(8,128)(2,1)} %param.6) | copy-start | bytes 3145732
  7.2 91.6 %all-gather.2.cloned.1.call-start = ((), (), s32[]{:S(2)}) async-start(), calls=%async_computation.3 | async-start | bytes 2162688 | tf_op jit(solution)/shard_map/all_gather | solution.py:20
  10.4 95.6 %all-to-all-start = ((bf16[32,32,1024]{2,1,0:T(8,128)(2,1)}), bf16[32,32,1024]{2,1,0:T(8,128)(2,1)S(1)}, u32[]{:S(2)}, u32[]{:S(2)}) async-start(bf16[32,32,1024]{2,1,0:T(8,128)(2,1)} %stack.2), calls=%async_computation.1 | async-start | bytes 4194304 | tf_op jit(solution)/shard_map/all_to_all | solution.py:39
  21.8 351.7 %all-reduce.3.cloned.1.call-start = ((), (), s32[]{:S(2)}) async-start(), calls=%async_computation.6 | async-start | bytes 12582912 | tf_op jit(solution)/shard_map/psum | solution.py:25
  98.8 3.3 copy-start.4
  105.9 4.6 copy-start.1
  110.5 402.5 %reduce-scatter.5.cloned.1.call-start = ((), (), s32[]{:S(2)}) async-start(), calls=%async_computation.5 | async-start | bytes 4325376 | tf_op jit(solution)/shard_map/reduce_scatter | solution.py:50
  377.8 1.3 copy-start.3
  377.8 1.6 copy-start.2
  382.7 260.6 %reduce-scatter.3.cloned.1.call-start = ((), (), s32[]{:S(2)}) async-start(), calls=%async_computation.4 | async-start | bytes 4325376 | tf_op jit(solution)/shard_map/reduce_scatter | solution.py:32
Sparse Core Ops, SparseCore 0:
  10.8 87.9 all-gather.1
  110.7 262.8 all-reduce.2
  382.8 130.1 reduce-scatter.4
  517.1 126.1 reduce-scatter.2
